TPU v7x, 128 devices: a whole 4x4x4 slice. The times are simulated.
128 devices in a mesh: sph: 16 (over y_hi, x, core), grp: 8 (over z, y_lo).
Axes of the slice: x: 4, y: 4 (y_hi: 2, y_lo: 2; y = y_hi * 2 + y_lo), z: 4, core: 2. Of those that a mesh axis runs over, the one named last changes fastest.
Arguments:
- pixel_features: bfloat16 [131072, 512], P(('sph', 'grp')), may hold values from -6 to 6
- tier_one_codes: bfloat16 [8192, 512], P(('sph', 'grp')), may hold values from -6 to 6
- tier_two_codes: bfloat16 [512, 512], P(('sph', 'grp')), may hold values from -6 to 6
- tier_three_codes: bfloat16 [32, 512], P('sph'), may hold values from -6 to 6
- tier_one_picks: int32 [8192, 16], P(('sph', 'grp')), may hold values from 0 to 8191, as said below
- tier_two_picks: int32 [8192, 16], P(('sph', 'grp')), may hold values from 0 to 511, as said below
- tier_three_picks: int32 [8192, 16], P(('sph', 'grp')), may hold values from 0 to 31, as said below
- probe_matrix: bfloat16 [3, 512, 512], replicated, may hold values from -0.25 to 0.25
- address_matrix: bfloat16 [3, 512, 512], replicated, may hold values from -0.25 to 0.25
- content_matrix: bfloat16 [3, 512, 512], replicated, may hold values from -0.25 to 0.25
- merge_matrix: bfloat16 [3, 512, 512], replicated, may hold values from -0.25 to 0.25
- expand_matrix: bfloat16 [3, 512, 1024], replicated, may hold values from -0.25 to 0.25
- shrink_matrix: bfloat16 [3, 1024, 512], replicated, may hold values from -0.1875 to 0.1875
- rescale_factors: float32 [3, 3, 512], replicated, may hold values from 0.25 to 1.75
- logit_scaling: float32 [3, 8], replicated, may hold values from 0.5 to 2
Outputs:
- encoded: bfloat16 [131072, 512], P(('sph', 'grp'))
Inputs may be any that keep to these rules, and one draw needn't show every extreme that they name: `tier_one_picks`: entry 0 of block b's list is b, its own level-one parent; every entry lies within 64 of b. `tier_two_picks`: entry 0 of block b's list is b // 16, its level-two parent; every entry lies in the same aligned run of 32 level-two latents as entry 0. `tier_three_picks`: entry 0 of block b's list is b // 256, its level-three parent.
All inputs are finite; a program needn't handle non-finite values.
Results may differ from a plain program's by a relative error of at most 0.01.
Values may be sent and summed in bfloat16 or wider, within the bound.
No kernel may reach another device: no remote copies, remote signals or barrier semaphores. Data moves between devices by JAX's collectives and lax.ppermute only.
A program may use at most 128 MiB of HBM per device.

v0:
```python
import math
import jax
import jax.numpy as jnp
from jax import lax
from jax.sharding import PartitionSpec as P

eps = 1e-06


def with_halo(block, sides, width):
    for axis, dim in sides:
        count = lax.axis_size(axis)
        forward = [(i, i + 1) for i in range(count - 1)]
        backward = [(target, source) for source, target in forward]
        low = lax.ppermute(
            lax.slice_in_dim(block, block.shape[dim] - width, None, axis=dim), axis, forward
        )
        high = lax.ppermute(lax.slice_in_dim(block, 0, width, axis=dim), axis, backward)
        block = jnp.concatenate([low, block, high], axis=dim)
    return block


def normalize(values_in, gain_vec):
    return (
        values_in
        * lax.rsqrt(jnp.mean(values_in * values_in, axis=-1, keepdims=True) + eps)
        * gain_vec
    )


def per_head(values_in, channel_groups):
    dims_shape = values_in.shape
    grouped = values_in.reshape(
        dims_shape[:-1] + (channel_groups, dims_shape[-1] // channel_groups)
    )
    grouped = grouped * lax.rsqrt(jnp.mean(grouped * grouped, axis=-1, keepdims=True) + eps)
    return grouped.reshape(dims_shape)


def refresh(latent, tier_ordinal, expand_matrix, shrink_matrix, rescale_factors):
    running_features = latent.astype(jnp.float32)
    mlp_in = normalize(running_features, rescale_factors[tier_ordinal, 1]).astype(jnp.bfloat16)
    hidden = jax.nn.silu(
        jnp.dot(mlp_in, expand_matrix[tier_ordinal], preferred_element_type=jnp.float32)
    ).astype(jnp.bfloat16)
    renewed = (
        running_features
        + jnp.dot(hidden, shrink_matrix[tier_ordinal], preferred_element_type=jnp.float32)
    ).astype(jnp.bfloat16)
    return lax.optimization_barrier(renewed)


def project(renewed, tier_ordinal, address_matrix, content_matrix, rescale_factors, channel_groups):
    kv_in = normalize(renewed.astype(jnp.float32), rescale_factors[tier_ordinal, 2]).astype(
        jnp.bfloat16
    )
    key_part = per_head(
        jnp.dot(kv_in, address_matrix[tier_ordinal], preferred_element_type=jnp.float32),
        channel_groups,
    ).astype(jnp.bfloat16)
    value_part = jnp.dot(
        kv_in, content_matrix[tier_ordinal], preferred_element_type=jnp.float32
    ).astype(jnp.bfloat16)
    return jnp.concatenate([key_part, value_part], axis=1)


def mix_across_tiers(
    running_features,
    gather_entries,
    tier_positions,
    tier_ordinal,
    probe_matrix,
    merge_matrix,
    rescale_factors,
    logit_scaling,
):
    row_count, feature = running_features.shape
    blocks = tier_positions.shape[0]
    channel_groups = logit_scaling.shape[1]
    group_dimension = feature // channel_groups
    table_rows = gather_entries.shape[0]
    normed = normalize(running_features, rescale_factors[tier_ordinal, 0]).astype(jnp.bfloat16)
    probe_heads = probe_matrix[tier_ordinal].reshape(feature, channel_groups, group_dimension)
    queries = jnp.einsum("rc,chd->hrd", normed, probe_heads, preferred_element_type=jnp.float32)
    queries = queries * lax.rsqrt(jnp.mean(queries * queries, axis=-1, keepdims=True) + eps)
    queries = queries.astype(jnp.bfloat16).reshape(
        channel_groups, blocks, row_count // blocks, group_dimension
    )
    key_heads = jnp.transpose(
        gather_entries[:, :feature].reshape(table_rows, channel_groups, group_dimension), (1, 0, 2)
    )
    value_heads = jnp.transpose(
        gather_entries[:, feature:].reshape(table_rows, channel_groups, group_dimension), (1, 0, 2)
    )
    key_picked = jnp.take(key_heads, tier_positions, axis=1)
    value_picked = jnp.take(value_heads, tier_positions, axis=1)
    affinity_logits = jnp.einsum(
        "hbid,hbjd->hbij", queries, key_picked, preferred_element_type=jnp.float32
    )
    affinity_logits = (
        affinity_logits
        * (logit_scaling[tier_ordinal] / math.sqrt(group_dimension))[:, None, None, None]
    )
    weights = jnp.exp(affinity_logits)
    weights = (weights / jnp.sum(weights, axis=-1, keepdims=True)).astype(jnp.bfloat16)
    mixture = jnp.einsum(
        "hbij,hbjd->hbid", weights, value_picked, preferred_element_type=jnp.float32
    )
    mixture = mixture.astype(jnp.bfloat16).reshape(channel_groups, row_count, group_dimension)
    merge_heads = merge_matrix[tier_ordinal].reshape(channel_groups, group_dimension, feature)
    return running_features + jnp.einsum(
        "hrd,hde->re", mixture, merge_heads, preferred_element_type=jnp.float32
    )


def per_device(
    pixel_features,
    tier_one_codes,
    tier_two_codes,
    tier_three_codes,
    tier_one_picks,
    tier_two_picks,
    tier_three_picks,
    probe_matrix,
    address_matrix,
    content_matrix,
    merge_matrix,
    expand_matrix,
    shrink_matrix,
    rescale_factors,
    logit_scaling,
):
    channel_groups = logit_scaling.shape[1]
    block_count = tier_one_codes.shape[0]
    device_index = lax.axis_index(("sph", "grp"))
    sphere_index = lax.axis_index("sph")
    renewed_one = refresh(tier_one_codes, 0, expand_matrix, shrink_matrix, rescale_factors)
    renewed_two = refresh(tier_two_codes, 1, expand_matrix, shrink_matrix, rescale_factors)
    renewed_three = refresh(tier_three_codes, 2, expand_matrix, shrink_matrix, rescale_factors)
    first_table = with_halo(
        project(renewed_one, 0, address_matrix, content_matrix, rescale_factors, channel_groups),
        ((("sph", "grp"), 0),),
        block_count,
    )
    second_table = lax.all_gather(
        project(renewed_two, 1, address_matrix, content_matrix, rescale_factors, channel_groups),
        "grp",
        axis=0,
        tiled=True,
    )
    third_table = lax.all_gather(
        project(renewed_three, 2, address_matrix, content_matrix, rescale_factors, channel_groups),
        "sph",
        axis=0,
        tiled=True,
    )
    local_first = tier_one_picks - (device_index * block_count - block_count)
    local_second = tier_two_picks - sphere_index * second_table.shape[0]
    running_features = pixel_features.astype(jnp.float32)
    running_features = mix_across_tiers(
        running_features,
        first_table,
        local_first,
        0,
        probe_matrix,
        merge_matrix,
        rescale_factors,
        logit_scaling,
    )
    running_features = mix_across_tiers(
        running_features,
        second_table,
        local_second,
        1,
        probe_matrix,
        merge_matrix,
        rescale_factors,
        logit_scaling,
    )
    running_features = mix_across_tiers(
        running_features,
        third_table,
        tier_three_picks,
        2,
        probe_matrix,
        merge_matrix,
        rescale_factors,
        logit_scaling,
    )
    return running_features.astype(jnp.bfloat16)


def solution(mesh):
    placed = (
        P(("sph", "grp"), None),
        P(("sph", "grp"), None),
        P(("sph", "grp"), None),
        P("sph", None),
        P(("sph", "grp"), None),
        P(("sph", "grp"), None),
        P(("sph", "grp"), None),
        P(),
        P(),
        P(),
        P(),
        P(),
        P(),
        P(),
        P(),
    )
    return jax.shard_map(
        per_device, mesh=mesh, in_specs=placed, out_specs=P(("sph", "grp"), None), check_vma=False
    )
```

profile of v0, /device:TPU:1, one launch (start us, length us, event | category | flops | bytes accessed | tf_op | source)
XLA Modules:
  0.0 174.7 jit_solution(10570810775063675648)
XLA Ops:
  0.0 1.5 fusion.159
  2.5 2.1 %fusion.35 = bf16[64,512]{1,0:T(8,128)(2,1)S(1)} fusion(bf16[3,1024,512]{2,1,0:T(8,128)(2,1)} %param.31, bf16[3,512,1024]{2,1,0:T(8,128)(2,1)} %param.30, bf16[64,512]{1,0:T(8,128)(2,1)} %param.20, f32[512]{0:T(512)S(1)} %bitcast.234, f32[64]{0:T(128)S(1)} %add_rsqrt_fusion.14), kind=kOutput, calls=%fused_computation.63 | convolution fusion | flops 134774784 | bytes 2296064 | tf_op jit(solution)/shard_map/dot_general | solution.py:48
  6.6 1.3 convolution_convert_fusion
  7.9 4.0 %collective-permute-start = (bf16[64,1024]{1,0:T(8,128)(2,1)S(1)}, bf16[64,1024]{1,0:T(8,128)(2,1)S(1)}, u32[]{:S(2)}, u32[]{:S(2)}) collective-permute-start(bf16[64,1024]{1,0:T(8,128)(2,1)S(1)} %pad_maximum_fusion.1), channel_id=1, source_target_pairs={{0,1},{1,2},{2,3},{3,4},{4,5},{5,6},{6,7},{7,8},{8,9},{9,10},{10,1... | collective-permute-start | bytes 393224 | tf_op jit(solution)/shard_map/ppermute | solution.py:15
  11.9 6.0 %collective-permute-start.1 = (bf16[64,1024]{1,0:T(8,128)(2,1)S(1)}, bf16[64,1024]{1,0:T(8,128)(2,1)}, u32[]{:S(2)}, u32[]{:S(2)}) collective-permute-start(bf16[64,1024]{1,0:T(8,128)(2,1)S(1)} %pad_maximum_fusion.1), channel_id=1, source_target_pairs={{1,0},{2,1},{3,2},{4,3},{5,4},{6,5},{7,6},{8,7},{9,8},{10,9},{11,1... | collective-permute-start | bytes 393224 | tf_op jit(solution)/shard_map/ppermute | solution.py:18
  20.2 1.9 %multiply_reduce_fusion.4 = (f32[8,1024]{1,0:T(8,128)S(1)}, f32[1024,512]{0,1:S(1)}) fusion(bf16[1024,512]{0,1:T(8,128)(2,1)S(1)} %copy.136, f32[512]{0:T(512)S(1)} %bitcast.233, f32[1024]{0:T(1024)S(1)} %add_rsqrt_fusion.8, bf16[3,512,512]{2,1,0:T(8,128)(2,1)} %param.26), kind=kOutput, calls=%fused_computation.54 | convolution fusion | flops 540008448 | bytes 3708928
  23.6 2.7 %fusion.155 = (bf16[1,512,512]{2,1,0:T(8,128)(2,1)}, bf16[1,512,512]{2,1,0:T(8,128)(2,1)}, bf16[1,512,512]{2,1,0:T(8,128)(2,1)}) fusion(bf16[3,512,512]{2,1,0:T(8,128)(2,1)} %param.29), kind=kLoop, calls=%fused_computation.208 | loop fusion | bytes 3145728 | tf_op jit(solution)/shard_map/slice | solution.py:110
  26.4 2.0 %fusion.36 = bf16[4,512]{1,0:T(4,128)(2,1)S(1)} fusion(bf16[3,1024,512]{2,1,0:T(8,128)(2,1)} %param.31, bf16[3,512,1024]{2,1,0:T(8,128)(2,1)} %param.30, bf16[4,512]{1,0:T(4,128)(2,1)S(1)} %copy-done.21, f32[512]{0:T(512)S(1)} %bitcast.232, f32[4]{0:T(128)S(1)} %add_rsqrt_fusion.12), kind=kOutput, calls=%fused_computation.66 | convolution fusion | flops 8423424 | bytes 2112000 | tf_op jit(solution)/shard_map/dot_general | solution.py:48
  31.8 22.1 %all-gather = bf16[8,4,1024]{2,1,0:T(4,128)(2,1)S(1)} all-gather(bf16[1,4,1024]{2,1,0:T(4,128)(2,1)S(1)} %maximum_bitcast_fusion), channel_id=1, replica_groups=mesh['sph'=16,'grp'=8] {'grp'}, dimensions={0}, use_global_device_ids=true | all-gather | bytes 73728 | tf_op jit(solution)/shard_map/all_gather | solution.py:145
  55.7 7.6 %gather_fusion.2 = bf16[1024,8,64]{2,1,0:T(8,128)(2,1)} fusion(bf16[8,32,64]{2,0,1:T(8,128)(2,1)S(1)} %bitcast.199, s32[1024]{0:T(1024)S(1)} %broadcast_clamp_fusion.1), kind=kCustom, calls=%fused_computation.1.clone | custom fusion | bytes 2101248 | tf_op jit(solution)/shard_map/jit(_take)/gather | solution.py:95
  63.4 7.6 %gather_fusion.3 = bf16[1024,8,64]{2,1,0:T(8,128)(2,1)} fusion(bf16[8,32,64]{2,0,1:T(8,128)(2,1)S(1)} %bitcast.201, s32[1024]{0:T(1024)S(1)} %broadcast_clamp_fusion.1), kind=kCustom, calls=%fused_computation.3.clone | custom fusion | bytes 2101248 | tf_op jit(solution)/shard_map/jit(_take)/gather | solution.py:96
  71.1 2.0 %fusion.37 = bf16[2,512]{1,0:T(2,128)(2,1)S(1)} fusion(bf16[3,1024,512]{2,1,0:T(8,128)(2,1)} %param.31, bf16[3,512,1024]{2,1,0:T(8,128)(2,1)} %param.30, bf16[2,512]{1,0:T(2,128)(2,1)S(1)} %copy-done.24, f32[2]{0:T(128)S(1)} %add_rsqrt_fusion.10, f32[512]{0:T(512)S(1)} %bitcast.231), kind=kOutput, calls=%fused_computation.69 | convolution fusion | flops 4211712 | bytes 2105856 | tf_op jit(solution)/shard_map/dot_general | solution.py:48
  76.5 30.7 %all-gather.1 = bf16[16,2,1024]{2,1,0:T(2,128)(2,1)S(1)} all-gather(bf16[1,2,1024]{2,1,0:T(2,128)(2,1)S(1)} %maximum_bitcast_fusion.1), channel_id=1, replica_groups=mesh['sph'=16,'grp'=8] {'sph'}, dimensions={0}, use_global_device_ids=true | all-gather | bytes 69632 | tf_op jit(solution)/shard_map/all_gather | solution.py:151
  108.3 1.4 copy.170
  109.7 7.6 %gather_fusion.4 = bf16[1024,8,64]{2,1,0:T(8,128)(2,1)} fusion(bf16[8,32,64]{2,0,1:T(8,128)(2,1)S(1)} %bitcast.200, s32[1024]{0:T(1024)S(1)} %broadcast_clamp_fusion), kind=kCustom, calls=%fused_computation.4.clone | custom fusion | bytes 2101248 | tf_op jit(solution)/shard_map/jit(_take)/gather | solution.py:95
  117.3 7.6 %gather_fusion.5 = bf16[1024,8,64]{2,1,0:T(8,128)(2,1)} fusion(bf16[8,32,64]{2,0,1:T(8,128)(2,1)S(1)} %bitcast.202, s32[1024]{0:T(1024)S(1)} %broadcast_clamp_fusion), kind=kCustom, calls=%fused_computation.5.clone | custom fusion | bytes 2101248 | tf_op jit(solution)/shard_map/jit(_take)/gather | solution.py:96
  127.2 7.6 %gather_fusion.1 = bf16[1024,8,64]{2,1,0:T(8,128)(2,1)} fusion(bf16[8,192,64]{2,0,1:T(8,128)(2,1)S(1)} %bitcast.203, s32[1024]{0:T(1024)S(1)} %broadcast_clamp_fusion.2), kind=kCustom, calls=%fused_computation.2.clone | custom fusion | bytes 2101248 | tf_op jit(solution)/shard_map/jit(_take)/gather | solution.py:96
  134.8 7.6 %gather_fusion = bf16[1024,8,64]{2,1,0:T(8,128)(2,1)} fusion(bf16[8,192,64]{2,0,1:T(8,128)(2,1)S(1)} %bitcast.204, s32[1024]{0:T(1024)S(1)} %broadcast_clamp_fusion.2), kind=kCustom, calls=%fused_computation.clone | custom fusion | bytes 2101248 | tf_op jit(solution)/shard_map/jit(_take)/gather | solution.py:95
  142.5 3.5 %select_bitcast_fusion.1 = (bf16[8,64,16,64]{3,0,2,1:T(8,128)(2,1)S(1)}, bf16[8,64,16,64]{3,0,2,1:T(8,128)(2,1)S(1)}) fusion(bf16[64,16,8,64]{3,2,1,0:T(8,128)(2,1)} %bitcast.207, pred[64,16]{1,0:T(8,128)(4,1)S(1)} %copy.140, bf16[64,16,8,64]{3,2,1,0:T(8,128)(2,1)} %bitcast.206), kind=kLoop, calls=%fused_computation.41 | loop fusion | flops 1048576 | bytes 4195328 | tf_op jit(solution)/shard_map/jit(_take)/select_n | solution.py:95
  146.0 1.4 fusion
  147.5 1.6 fusion.26
  149.2 1.3 multiply_reduce_fusion.3
  150.5 2.3 %multiply_reduce_fusion.2 = (f32[8,1024]{1,0:T(8,128)S(1)}, f32[1024,512]{0,1:S(1)}) fusion(f32[1024,512]{0,1:T(8,128)S(1)} %get-tuple-element.46, f32[512]{0:T(512)S(1)} %bitcast.224, f32[1024]{0:T(1024)S(1)} %add_rsqrt_fusion.6, bf16[3,512,512]{2,1,0:T(8,128)(2,1)} %param.26), kind=kOutput, calls=%fused_computation.49 | convolution fusion | flops 539484160 | bytes 4757504
  154.2 4.3 %fusion.1 = (f32[8,64,16]{2,1,0:T(8,128)S(1)}, f32[8,64,16,16]{2,3,1,0:T(8,128)S(1)}) fusion(f32[8]{0:T(128)S(1)} %copy-done.27, bf16[8,64,16,64]{3,2,1,0:T(8,128)(2,1)S(1)} %bitcast.209, bf16[64,16,8,64]{3,2,1,0:T(8,128)(2,1)} %bitcast.212, pred[64,16]{1,0:T(8,128)(4,1)S(1)} %copy-done.19), kind=kOutput, calls=%fused_computation.13 | convolution fusion | flops 17555456 | bytes 2655264 | tf_op jit(solution)/shard_map/hbid,hbjd->hbij/dot_general | solution.py:97
  158.6 2.1 %fusion.29 = bf16[8,64,16,64]{3,2,1,0:T(8,128)(2,1)S(1)} fusion(bf16[64,16,8,64]{3,2,1,0:T(8,128)(2,1)S(1)} %bitcast.211, pred[64,16]{1,0:T(8,128)(4,1)S(1)} %copy-done.19, f32[8,64,16,16]{2,3,1,0:T(8,128)S(1)} %get-tuple-element.50, f32[8,64,16]{2,1,0:T(8,128)S(1)} %get-tuple-element.49, f32[8]{0:T(128)S(1)} %copy-done.27), kind=kOutput, calls=%fused_computation.60 | convolution fusion | flops 18219008 | bytes 2655264 | tf_op jit(solution)/shard_map/hbij,hbjd->hbid/dot_general | solution.py:106
  160.7 1.3 multiply_reduce_fusion.1
  162.1 1.9 %multiply_reduce_fusion = (f32[8,1024]{1,0:T(8,128)S(1)}, f32[1024,512]{0,1:S(1)}) fusion(f32[1024,512]{0,1:T(8,128)S(1)} %get-tuple-element.54, f32[512]{0:T(512)S(1)} %bitcast.223, f32[1024]{0:T(1024)S(1)} %add_rsqrt_fusion.4, bf16[3,512,512]{2,1,0:T(8,128)(2,1)} %param.26), kind=kOutput, calls=%fused_computation.44 | convolution fusion | flops 539484160 | bytes 4757504
  164.2 1.8 %copy.169 = bf16[8,1024,64]{2,1,0:T(8,128)(2,1)} copy(bf16[8,1024,64]{1,2,0:T(8,128)(2,1)S(1)} %multiply_convert_fusion) | data formatting | bytes 2097152 | tf_op jit(solution)/shard_map/convert_element_type | solution.py:86
  166.1 3.9 %fusion.2 = (f32[8,64,16]{2,1,0:T(8,128)S(1)}, f32[8,64,16,16]{2,3,1,0:T(8,128)S(1)}) fusion(f32[8]{0:T(128)S(1)} %copy-done.26, bf16[8,64,16,64]{3,2,1,0:T(8,128)(2,1)} %bitcast.208, bf16[64,16,8,64]{3,2,1,0:T(8,128)(2,1)} %bitcast.214, pred[64,16]{1,0:T(8,128)(4,1)S(1)} %copy-done.20), kind=kOutput, calls=%fused_computation.14 | convolution fusion | flops 17555456 | bytes 2655264 | tf_op jit(solution)/shard_map/hbid,hbjd->hbij/dot_general | solution.py:97
  170.0 2.1 %fusion.32 = bf16[8,64,16,64]{3,2,1,0:T(8,128)(2,1)S(1)} fusion(bf16[64,16,8,64]{3,2,1,0:T(8,128)(2,1)S(1)} %bitcast.213, pred[64,16]{1,0:T(8,128)(4,1)S(1)} %copy-done.20, f32[8,64,16,16]{2,3,1,0:T(8,128)S(1)} %get-tuple-element.58, f32[8,64,16]{2,1,0:T(8,128)S(1)} %get-tuple-element.57, f32[8]{0:T(128)S(1)} %copy-done.26), kind=kOutput, calls=%fused_computation.61 | convolution fusion | flops 18219008 | bytes 2655264 | tf_op jit(solution)/shard_map/hbij,hbjd->hbid/dot_general | solution.py:106
  172.1 1.3 fusion.6
  173.4 1.3 copy.181
  (136 shorter events, 20.5 us)
Async XLA Ops:
  0.0 4.8 %copy-start.8 = (bf16[3,512,512]{2,1,0:T(8,128)(2,1)S(1)}, bf16[3,512,512]{2,1,0:T(8,128)(2,1)}, u32[]{:S(2)}) copy-start(bf16[3,512,512]{2,1,0:T(8,128)(2,1)} %param.27) | copy-start | bytes 4718596
  5.9 12.1 %copy-start.13 = (s32[64,16]{0,1:T(8,128)S(1)}, s32[64,16]{0,1:T(8,128)}, u32[]{:S(2)}) copy-start(s32[64,16]{0,1:T(8,128)} %param.25) | copy-start | bytes 12292
  5.9 13.2 %copy-start.18 = (s32[64,16]{0,1:T(8,128)S(1)}, s32[64,16]{0,1:T(8,128)}, u32[]{:S(2)}) copy-start(s32[64,16]{0,1:T(8,128)} %param.23) | copy-start | bytes 12292
  5.9 13.5 %copy-start.9 = (bf16[1024,512]{1,0:T(8,128)(2,1)S(1)}, bf16[1024,512]{1,0:T(8,128)(2,1)}, u32[]{:S(2)}) copy-start(bf16[1024,512]{1,0:T(8,128)(2,1)} %param.19) | copy-start | bytes 3145732
  7.9 117.6 %collective-permute-start = (bf16[64,1024]{1,0:T(8,128)(2,1)S(1)}, bf16[64,1024]{1,0:T(8,128)(2,1)S(1)}, u32[]{:S(2)}, u32[]{:S(2)}) collective-permute-start(bf16[64,1024]{1,0:T(8,128)(2,1)S(1)} %pad_maximum_fusion.1), channel_id=1, source_target_pairs={{0,1},{1,2},{2,3},{3,4},{4,5},{5,6},{6,7},{7,8},{8,9},{9,10},{10,1... | collective-permute-start | bytes 393224 | tf_op jit(solution)/shard_map/ppermute | solution.py:15
  11.9 113.5 %collective-permute-start.1 = (bf16[64,1024]{1,0:T(8,128)(2,1)S(1)}, bf16[64,1024]{1,0:T(8,128)(2,1)}, u32[]{:S(2)}, u32[]{:S(2)}) collective-permute-start(bf16[64,1024]{1,0:T(8,128)(2,1)S(1)} %pad_maximum_fusion.1), channel_id=1, source_target_pairs={{1,0},{2,1},{3,2},{4,3},{5,4},{6,5},{7,6},{8,7},{9,8},{10,9},{11,1... | collective-permute-start | bytes 393224 | tf_op jit(solution)/shard_map/ppermute | solution.py:18
  19.9 2.2 %copy-start = (bf16[1024,512]{0,1:T(8,128)(2,1)}, bf16[1024,512]{0,1:T(8,128)(2,1)S(1)}, u32[]{:S(2)}) copy-start(bf16[1024,512]{0,1:T(8,128)(2,1)S(1)} %copy.136) | copy-start | bytes 3145732
  23.5 2.7 %copy-start.21 = (bf16[4,512]{1,0:T(4,128)(2,1)S(1)}, bf16[4,512]{1,0:T(4,128)(2,1)}, u32[]{:S(2)}) copy-start(bf16[4,512]{1,0:T(4,128)(2,1)} %param.21) | copy-start | bytes 12292
  23.6 2.8 %copy-start.23 = (f32[1,1,512]{2,1,0:T(1,128)S(1)}, f32[1,1,512]{2,1,0:T(1,128)}, u32[]{:S(2)}) copy-start(f32[1,1,512]{2,1,0:T(1,128)} %get-tuple-element.25) | copy-start | bytes 6148
  23.6 5.4 %copy-start.7 = (bf16[512,512]{0,1:T(8,128)(2,1)S(1)}, bf16[512,512]{0,1:T(8,128)(2,1)}, u32[]{:S(2)}) copy-start(bf16[512,512]{0,1:T(8,128)(2,1)} %get-tuple-element.16) | copy-start | bytes 1572868
  63.4 7.6 %copy-start.24 = (bf16[2,512]{1,0:T(2,128)(2,1)S(1)}, bf16[2,512]{1,0:T(2,128)(2,1)}, u32[]{:S(2)}) copy-start(bf16[2,512]{1,0:T(2,128)(2,1)} %param.22) | copy-start | bytes 6148
  63.4 7.7 %copy-start.22 = (f32[1,1,512]{2,1,0:T(1,128)S(1)}, f32[1,1,512]{2,1,0:T(1,128)}, u32[]{:S(2)}) copy-start(f32[1,1,512]{2,1,0:T(1,128)} %get-tuple-element.31) | copy-start | bytes 6148
  71.0 2.8 %copy-start.6 = (bf16[512,512]{0,1:T(8,128)(2,1)S(1)}, bf16[512,512]{0,1:T(8,128)(2,1)}, u32[]{:S(2)}) copy-start(bf16[512,512]{0,1:T(8,128)(2,1)} %get-tuple-element.14) | copy-start | bytes 1572868
  71.0 3.0 %copy-start.16 = (f32[1,1,512]{2,1,0:T(1,128)S(1)}, f32[1,1,512]{2,1,0:T(1,128)}, u32[]{:S(2)}) copy-start(f32[1,1,512]{2,1,0:T(1,128)} %get-tuple-element.30) | copy-start | bytes 6148
  73.1 0.7 copy-start.17
  117.3 7.6 %copy-start.25 = (f32[3,8]{1,0:T(4,128)S(1)}, f32[3,8]{1,0:T(4,128)}, u32[]{:S(2)}) copy-start(f32[3,8]{1,0:T(4,128)} %param.33) | copy-start | bytes 292
  147.4 1.7 copy-start.1
  147.5 1.7 copy-start.12
  149.1 1.4 copy-start.15
  150.5 2.3 %copy-start.2 = (f32[1024,512]{0,1:T(8,128)}, f32[1024,512]{0,1:T(8,128)S(1)}, u32[]{:S(2)}) copy-start(f32[1024,512]{0,1:T(8,128)S(1)} %get-tuple-element.46) | copy-start | bytes 6291460
  153.1 1.1 copy-start.19
  153.1 1.1 copy-start.27
  154.2 4.3 %copy-start.4 = (bf16[1024,8,64]{2,1,0:T(8,128)(2,1)S(1)}, bf16[1024,8,64]{2,1,0:T(8,128)(2,1)}, u32[]{:S(2)}) copy-start(bf16[1024,8,64]{2,1,0:T(8,128)(2,1)} %gather_fusion.3) | copy-start | bytes 3145732
  158.6 2.1 %copy-start.3 = (f32[1024,512]{0,1:T(8,128)S(1)}, f32[1024,512]{0,1:T(8,128)}, u32[]{:S(2)}) copy-start(f32[1024,512]{0,1:T(8,128)} %copy-done.2) | copy-start | bytes 6291460
  158.6 2.1 %copy-start.11 = (bf16[1,512,512]{2,1,0:T(8,128)(2,1)S(1)}, bf16[1,512,512]{2,1,0:T(8,128)(2,1)}, u32[]{:S(2)}) copy-start(bf16[1,512,512]{2,1,0:T(8,128)(2,1)} %get-tuple-element.13) | copy-start | bytes 1572868
  160.7 1.4 copy-start.14
  164.2 1.9 %copy-start.20 = (pred[64,16]{1,0:T(8,128)(4,1)S(1)}, pred[64,16]{1,0:T(8,128)(4,1)}, u32[]{:S(2)}) copy-start(pred[64,16]{1,0:T(8,128)(4,1)} %copy.170) | copy-start | bytes 3076
  164.2 1.8 %copy-start.26 = (f32[8]{0:T(128)S(1)}, f32[8]{0:T(128)}, u32[]{:S(2)}) copy-start(f32[8]{0:T(128)} %get-tuple-element.34) | copy-start | bytes 100
  166.1 3.9 %copy-start.5 = (bf16[1024,8,64]{2,1,0:T(8,128)(2,1)S(1)}, bf16[1024,8,64]{2,1,0:T(8,128)(2,1)}, u32[]{:S(2)}) copy-start(bf16[1024,8,64]{2,1,0:T(8,128)(2,1)} %gather_fusion.5) | copy-start | bytes 3145732
  170.0 2.1 %copy-start.10 = (bf16[1,512,512]{2,1,0:T(8,128)(2,1)S(1)}, bf16[1,512,512]{2,1,0:T(8,128)(2,1)}, u32[]{:S(2)}) copy-start(bf16[1,512,512]{2,1,0:T(8,128)(2,1)} %get-tuple-element.11) | copy-start | bytes 1572868
where the time goes:
time: 176 us; the launch traced here: 175 us
  local copies, waits for them, and re-layouts  62.3 us (35%)
  blocking collectives  52.8 us (30%)
  matrix products  37.9 us (22%)
  other arithmetic  11 us (6%)
  starting transfers between devices  9.98 us (6%)
    all_gather x1, blocking collectives, per_device(): lax.all_gather(project(renewed_three, 2, address_matrix, content_matrix,...  30.7 us
    gather x3, local copies, waits for them, and re-layouts, mix_across_tiers(): key_picked = jnp.take(key_heads, tier_positions, axis=1)  22.8 us
    gather x3, local copies, waits for them, and re-layouts, mix_across_tiers(): value_picked = jnp.take(value_heads, tier_positions, axis=1)  22.8 us
    all_gather x1, blocking collectives, per_device(): lax.all_gather(project(renewed_two, 1, address_matrix, content_matrix, re...  22.1 us
    dot_general x3, matrix products, mix_across_tiers(): jnp.einsum('hbid,hbjd->hbij', queries, key_picked, preferred_element_type...  9.67 us
    dot_general x3, matrix products, refresh(): jnp.dot(hidden, shrink_matrix[tier_ordinal], preferred_element_type=jnp.f...  6.09 us
    unnamed x3, matrix products  6.07 us
    ppermute x1, starting transfers between devices, with_halo(): lax.ppermute(lax.slice_in_dim(block, 0, width, axis=dim), axis, backward)  5.96 us
  transfers between devices with their start and end apart: 2, of which 0 were waited for; matrix products, arithmetic and copies ran while one was open for 31% of the time, Pallas kernels for 0%

commit v1 on v0

--- a/solution.py
+++ b/solution.py
@@ -142,11 +142,26 @@
         ((("sph", "grp"), 0),),
         block_count,
     )
-    second_table = lax.all_gather(
-        project(renewed_two, 1, address_matrix, content_matrix, rescale_factors, channel_groups),
-        "grp",
+    second_table = jnp.concatenate(
+        lax.all_to_all(
+            jnp.stack(
+                [
+                    project(
+                        renewed_two,
+                        1,
+                        address_matrix,
+                        content_matrix,
+                        rescale_factors,
+                        channel_groups,
+                    )
+                ]
+                * lax.axis_size("grp")
+            ),
+            "grp",
+            0,
+            0,
+        ),
         axis=0,
-        tiled=True,
     )
     third_table = lax.all_gather(
         project(renewed_three, 2, address_matrix, content_matrix, rescale_factors, channel_groups),

time: 176 us -> 153 us (0.87)
  blocking collectives: 52.8 us -> 24.7 us
  starting transfers between devices: 9.98 us -> 13.3 us
    all_gather x1 -> x0, blocking collectives: 22.1 us -> none  [per_device(): lax.all_gather(project(renewed_two, 1, address_matrix, content_matrix, re...]
    all_gather x1, blocking collectives: 30.7 us -> 24.7 us  [per_device(): lax.all_gather(project(renewed_three, 2, address_matrix, content_matrix,...]
    all_to_all x0 -> x1, starting transfers between devices: none -> 3.35 us  [per_device(): lax.all_to_all(jnp.stack([project(renewed_two, 1, address_matrix, content...]
  transfers between devices with their start and end apart: 2 -> 3, of which waited for: 0 -> 0; matrix products, arithmetic and copies ran while one was open for 31% -> 37% of each run, Pallas kernels for 0% -> 0%
where the time goes in v1:
time: 153 us; the launch traced here: 152 us
  local copies, waits for them, and re-layouts  63.8 us (42%)
  matrix products  38.3 us (25%)
  blocking collectives  24.7 us (16%)
  starting transfers between devices  13.3 us (9%)
  other arithmetic  11.3 us (7%)
    all_gather x1, blocking collectives, per_device(): lax.all_gather(project(renewed_three, 2, address_matrix, content_matrix,...  24.7 us
    gather x3, local copies, waits for them, and re-layouts, mix_across_tiers(): key_picked = jnp.take(key_heads, tier_positions, axis=1)  22.8 us
    gather x3, local copies, waits for them, and re-layouts, mix_across_tiers(): value_picked = jnp.take(value_heads, tier_positions, axis=1)  22.8 us
    dot_general x3, matrix products, mix_across_tiers(): jnp.einsum('hbid,hbjd->hbij', queries, key_picked, preferred_element_type...  9.67 us
    unnamed x3, matrix products  7.44 us
    dot_general x3, matrix products, refresh(): jnp.dot(hidden, shrink_matrix[tier_ordinal], preferred_element_type=jnp.f...  6.3 us
    dot_general x3, matrix products, mix_across_tiers(): jnp.einsum('hbij,hbjd->hbid', weights, value_picked, preferred_element_ty...  6.02 us
    ppermute x1, starting transfers between devices, with_halo(): lax.ppermute(lax.slice_in_dim(block, 0, width, axis=dim), axis, backward)  5.95 us
  transfers between devices with their start and end apart: 3, of which 0 were waited for; matrix products, arithmetic and copies ran while one was open for 37% of the time, Pallas kernels for 0%

profile of v1, /device:TPU:1, one launch (start us, length us, event | category | flops | bytes accessed | tf_op | source)
XLA Modules:
  0.0 152.1 jit_solution(9792574985340904014)
XLA Ops:
  0.0 1.4 fusion.159
  2.4 2.1 %fusion.35 = bf16[64,512]{1,0:T(8,128)(2,1)S(1)} fusion(bf16[3,1024,512]{2,1,0:T(8,128)(2,1)} %param.31, bf16[3,512,1024]{2,1,0:T(8,128)(2,1)} %param.30, bf16[64,512]{1,0:T(8,128)(2,1)} %param.20, f32[512]{0:T(512)S(1)} %bitcast.232, f32[64]{0:T(128)S(1)} %add_rsqrt_fusion.14), kind=kOutput, calls=%fused_computation.63 | convolution fusion | flops 134774784 | bytes 2296064 | tf_op jit(solution)/shard_map/dot_general | solution.py:48
  4.6 1.5 slice_bitcast_fusion
  8.2 4.0 %collective-permute-start = (bf16[64,1024]{1,0:T(8,128)(2,1)S(1)}, bf16[64,1024]{1,0:T(8,128)(2,1)}, u32[]{:S(2)}, u32[]{:S(2)}) collective-permute-start(bf16[64,1024]{1,0:T(8,128)(2,1)S(1)} %pad_maximum_fusion.1), channel_id=1, source_target_pairs={{0,1},{1,2},{2,3},{3,4},{4,5},{5,6},{6,7},{7,8},{8,9},{9,10},{10,1... | collective-permute-start | bytes 393224 | tf_op jit(solution)/shard_map/ppermute | solution.py:15
  12.2 6.0 %collective-permute-start.1 = (bf16[64,1024]{1,0:T(8,128)(2,1)S(1)}, bf16[64,1024]{1,0:T(8,128)(2,1)}, u32[]{:S(2)}, u32[]{:S(2)}) collective-permute-start(bf16[64,1024]{1,0:T(8,128)(2,1)S(1)} %pad_maximum_fusion.1), channel_id=1, source_target_pairs={{1,0},{2,1},{3,2},{4,3},{5,4},{6,5},{7,6},{8,7},{9,8},{10,9},{11,1... | collective-permute-start | bytes 393224 | tf_op jit(solution)/shard_map/ppermute | solution.py:18
  18.3 2.1 %fusion.36 = bf16[4,512]{1,0:T(4,128)(2,1)S(1)} fusion(bf16[3,1024,512]{2,1,0:T(8,128)(2,1)} %param.31, bf16[3,512,1024]{2,1,0:T(8,128)(2,1)} %param.30, bf16[4,512]{1,0:T(4,128)(2,1)S(1)} %copy-done.19, f32[512]{0:T(512)S(1)} %bitcast.231, f32[4]{0:T(128)S(1)} %add_rsqrt_fusion.12), kind=kOutput, calls=%fused_computation.66 | convolution fusion | flops 8423424 | bytes 2112000 | tf_op jit(solution)/shard_map/dot_general | solution.py:48
  23.3 3.3 %all-to-all-start = ((bf16[8,4,1024]{2,1,0:T(4,128)(2,1)}), bf16[8,4,1024]{2,1,0:T(4,128)(2,1)S(1)}, u32[]{:S(2)}, u32[]{:S(2)}) async-start(bf16[8,4,1024]{2,1,0:T(4,128)(2,1)} %stack.2), calls=%async_computation | async-start | bytes 131072 | tf_op jit(solution)/shard_map/all_to_all | solution.py:146
  29.5 3.3 %multiply_reduce_fusion.4 = (f32[8,1024]{1,0:T(8,128)S(1)}, f32[1024,512]{0,1}) fusion(bf16[1024,512]{0,1:T(8,128)(2,1)S(1)} %copy.136, f32[512]{0:T(512)S(1)} %bitcast.230, f32[1024]{0:T(1024)S(1)} %add_rsqrt_fusion.8, bf16[3,512,512]{2,1,0:T(8,128)(2,1)} %param.26), kind=kOutput, calls=%fused_computation.54 | convolution fusion | flops 540008448 | bytes 3708928
  35.0 2.1 %fusion.37 = bf16[2,512]{1,0:T(2,128)(2,1)S(1)} fusion(bf16[3,1024,512]{2,1,0:T(8,128)(2,1)} %param.31, bf16[3,512,1024]{2,1,0:T(8,128)(2,1)} %param.30, bf16[2,512]{1,0:T(2,128)(2,1)S(1)} %copy-done.21, f32[2]{0:T(128)S(1)} %add_rsqrt_fusion.10, f32[512]{0:T(512)S(1)} %bitcast.229), kind=kOutput, calls=%fused_computation.69 | convolution fusion | flops 4211712 | bytes 2105856 | tf_op jit(solution)/shard_map/dot_general | solution.py:48
  39.4 24.7 %all-gather = bf16[16,2,1024]{2,1,0:T(2,128)(2,1)S(1)} all-gather(bf16[1,2,1024]{2,1,0:T(2,128)(2,1)S(1)} %maximum_bitcast_fusion), channel_id=1, replica_groups=mesh['sph'=16,'grp'=8] {'sph'}, dimensions={0}, use_global_device_ids=true | all-gather | bytes 69632 | tf_op jit(solution)/shard_map/all_gather | solution.py:166
  65.9 1.4 multiply_bitcast_fusion
  67.2 1.4 copy.140
  69.6 1.4 copy.157
  72.0 7.6 %gather_fusion.4 = bf16[1024,8,64]{2,1,0:T(8,128)(2,1)} fusion(bf16[8,32,64]{2,0,1:T(8,128)(2,1)S(1)} %bitcast.197, s32[1024]{0:T(1024)S(1)} %broadcast_clamp_fusion), kind=kCustom, calls=%fused_computation.4.clone | custom fusion | bytes 2101248 | tf_op jit(solution)/shard_map/jit(_take)/gather | solution.py:95
  79.6 7.6 %gather_fusion.5 = bf16[1024,8,64]{2,1,0:T(8,128)(2,1)} fusion(bf16[8,32,64]{2,0,1:T(8,128)(2,1)S(1)} %bitcast.198, s32[1024]{0:T(1024)S(1)} %broadcast_clamp_fusion), kind=kCustom, calls=%fused_computation.5.clone | custom fusion | bytes 2101248 | tf_op jit(solution)/shard_map/jit(_take)/gather | solution.py:96
  87.4 7.6 %gather_fusion.2 = bf16[1024,8,64]{2,1,0:T(8,128)(2,1)} fusion(bf16[8,32,64]{2,0,1:T(8,128)(2,1)S(1)} %bitcast.199, s32[1024]{0:T(1024)S(1)} %broadcast_clamp_fusion.1), kind=kCustom, calls=%fused_computation.1.clone | custom fusion | bytes 2101248 | tf_op jit(solution)/shard_map/jit(_take)/gather | solution.py:95
  95.0 7.6 %gather_fusion.3 = bf16[1024,8,64]{2,1,0:T(8,128)(2,1)} fusion(bf16[8,32,64]{2,0,1:T(8,128)(2,1)S(1)} %bitcast.200, s32[1024]{0:T(1024)S(1)} %broadcast_clamp_fusion.1), kind=kCustom, calls=%fused_computation.3.clone | custom fusion | bytes 2101248 | tf_op jit(solution)/shard_map/jit(_take)/gather | solution.py:96
  104.4 7.6 %gather_fusion.1 = bf16[1024,8,64]{2,1,0:T(8,128)(2,1)} fusion(bf16[8,192,64]{2,0,1:T(8,128)(2,1)S(1)} %bitcast.201, s32[1024]{0:T(1024)S(1)} %broadcast_clamp_fusion.2), kind=kCustom, calls=%fused_computation.2.clone | custom fusion | bytes 2101248 | tf_op jit(solution)/shard_map/jit(_take)/gather | solution.py:96
  112.0 7.6 %gather_fusion = bf16[1024,8,64]{2,1,0:T(8,128)(2,1)} fusion(bf16[8,192,64]{2,0,1:T(8,128)(2,1)S(1)} %bitcast.202, s32[1024]{0:T(1024)S(1)} %broadcast_clamp_fusion.2), kind=kCustom, calls=%fused_computation.clone | custom fusion | bytes 2101248 | tf_op jit(solution)/shard_map/jit(_take)/gather | solution.py:95
  119.7 3.5 %select_bitcast_fusion.1 = (bf16[8,64,16,64]{3,0,2,1:T(8,128)(2,1)S(1)}, bf16[8,64,16,64]{3,0,2,1:T(8,128)(2,1)S(1)}) fusion(bf16[64,16,8,64]{3,2,1,0:T(8,128)(2,1)} %bitcast.205, pred[64,16]{1,0:T(8,128)(4,1)S(1)} %copy-done.13, bf16[64,16,8,64]{3,2,1,0:T(8,128)(2,1)} %bitcast.204), kind=kLoop, calls=%fused_computation.41 | loop fusion | flops 1048576 | bytes 4195328 | tf_op jit(solution)/shard_map/jit(_take)/select_n | solution.py:95
  123.2 1.4 fusion
  124.7 1.6 %fusion.26 = bf16[8,64,16,64]{3,2,1,0:T(8,128)(2,1)S(1)} fusion(bf16[8,64,16,64]{3,0,2,1:T(8,128)(2,1)S(1)} %get-tuple-element.33, f32[8,64,16,16]{2,3,1,0:T(8,128)S(1)} %get-tuple-element.42, f32[8,64,16]{2,1,0:T(8,128)S(1)} %get-tuple-element.41, f32[8]{0:T(128)S(1)} %copy-done.20), kind=kOutput, calls=%fused_computation.59 | convolution fusion | flops 17694720 | bytes 2654240 | tf_op jit(solution)/shard_map/hbij,hbjd->hbid/dot_general | solution.py:106
  126.4 1.3 multiply_reduce_fusion.3
  127.8 2.3 %multiply_reduce_fusion.2 = (f32[8,1024]{1,0:T(8,128)S(1)}, f32[1024,512]{0,1:S(1)}) fusion(f32[1024,512]{0,1:T(8,128)S(1)} %get-tuple-element.46, f32[512]{0:T(512)S(1)} %bitcast.222, f32[1024]{0:T(1024)S(1)} %add_rsqrt_fusion.6, bf16[3,512,512]{2,1,0:T(8,128)(2,1)} %param.26), kind=kOutput, calls=%fused_computation.49 | convolution fusion | flops 539484160 | bytes 4757504
  131.5 4.3 %fusion.1 = (f32[8,64,16]{2,1,0:T(8,128)S(1)}, f32[8,64,16,16]{2,3,1,0:T(8,128)S(1)}) fusion(f32[8]{0:T(128)S(1)} %copy-done.23, bf16[8,64,16,64]{3,2,1,0:T(8,128)(2,1)S(1)} %bitcast.207, bf16[64,16,8,64]{3,2,1,0:T(8,128)(2,1)} %bitcast.212, pred[64,16]{1,0:T(8,128)(4,1)S(1)} %copy-done.18), kind=kOutput, calls=%fused_computation.13 | convolution fusion | flops 17555456 | bytes 2655264 | tf_op jit(solution)/shard_map/hbid,hbjd->hbij/dot_general | solution.py:97
  135.8 2.3 %fusion.29 = bf16[8,64,16,64]{3,2,1,0:T(8,128)(2,1)S(1)} fusion(bf16[64,16,8,64]{3,2,1,0:T(8,128)(2,1)S(1)} %bitcast.211, pred[64,16]{1,0:T(8,128)(4,1)S(1)} %copy-done.18, f32[8,64,16,16]{2,3,1,0:T(8,128)S(1)} %get-tuple-element.50, f32[8,64,16]{2,1,0:T(8,128)S(1)} %get-tuple-element.49, f32[8]{0:T(128)S(1)} %copy-done.23), kind=kOutput, calls=%fused_computation.60 | convolution fusion | flops 18219008 | bytes 2655264 | tf_op jit(solution)/shard_map/hbij,hbjd->hbid/dot_general | solution.py:106
  138.1 1.3 multiply_reduce_fusion.1
  139.5 1.9 %multiply_reduce_fusion = (f32[8,1024]{1,0:T(8,128)S(1)}, f32[1024,512]{0,1:S(1)}) fusion(f32[1024,512]{0,1:T(8,128)S(1)} %get-tuple-element.54, f32[512]{0:T(512)S(1)} %bitcast.221, f32[1024]{0:T(1024)S(1)} %add_rsqrt_fusion.4, bf16[3,512,512]{2,1,0:T(8,128)(2,1)} %param.26), kind=kOutput, calls=%fused_computation.44 | convolution fusion | flops 539484160 | bytes 4757504
  141.7 1.8 %copy.169 = bf16[8,1024,64]{2,1,0:T(8,128)(2,1)} copy(bf16[8,1024,64]{1,2,0:T(8,128)(2,1)S(1)} %multiply_convert_fusion) | data formatting | bytes 2097152 | tf_op jit(solution)/shard_map/convert_element_type | solution.py:86
  143.5 3.9 %fusion.2 = (f32[8,64,16]{2,1,0:T(8,128)S(1)}, f32[8,64,16,16]{2,3,1,0:T(8,128)S(1)}) fusion(f32[8]{0:T(128)S(1)} %copy-done.22, bf16[8,64,16,64]{3,2,1,0:T(8,128)(2,1)} %bitcast.206, bf16[64,16,8,64]{3,2,1,0:T(8,128)(2,1)} %bitcast.210, pred[64,16]{1,0:T(8,128)(4,1)S(1)} %copy.170), kind=kOutput, calls=%fused_computation.14 | convolution fusion | flops 17555456 | bytes 2655264 | tf_op jit(solution)/shard_map/hbid,hbjd->hbij/dot_general | solution.py:97
  147.4 2.1 %fusion.32 = bf16[8,64,16,64]{3,2,1,0:T(8,128)(2,1)S(1)} fusion(bf16[64,16,8,64]{3,2,1,0:T(8,128)(2,1)S(1)} %bitcast.209, pred[64,16]{1,0:T(8,128)(4,1)S(1)} %copy.170, f32[8,64,16,16]{2,3,1,0:T(8,128)S(1)} %get-tuple-element.58, f32[8,64,16]{2,1,0:T(8,128)S(1)} %get-tuple-element.57, f32[8]{0:T(128)S(1)} %copy-done.22), kind=kOutput, calls=%fused_computation.61 | convolution fusion | flops 18219008 | bytes 2655264 | tf_op jit(solution)/shard_map/hbij,hbjd->hbid/dot_general | solution.py:106
  150.8 1.3 copy.181
  (130 shorter events, 22.1 us)
Async XLA Ops:
  6.1 12.1 %copy-start.19 = (bf16[4,512]{1,0:T(4,128)(2,1)S(1)}, bf16[4,512]{1,0:T(4,128)(2,1)}, u32[]{:S(2)}) copy-start(bf16[4,512]{1,0:T(4,128)(2,1)} %param.21) | copy-start | bytes 12292
  8.2 94.4 %collective-permute-start = (bf16[64,1024]{1,0:T(8,128)(2,1)S(1)}, bf16[64,1024]{1,0:T(8,128)(2,1)}, u32[]{:S(2)}, u32[]{:S(2)}) collective-permute-start(bf16[64,1024]{1,0:T(8,128)(2,1)S(1)} %pad_maximum_fusion.1), channel_id=1, source_target_pairs={{0,1},{1,2},{2,3},{3,4},{4,5},{5,6},{6,7},{7,8},{8,9},{9,10},{10,1... | collective-permute-start | bytes 393224 | tf_op jit(solution)/shard_map/ppermute | solution.py:15
  12.2 90.4 %collective-permute-start.1 = (bf16[64,1024]{1,0:T(8,128)(2,1)S(1)}, bf16[64,1024]{1,0:T(8,128)(2,1)}, u32[]{:S(2)}, u32[]{:S(2)}) collective-permute-start(bf16[64,1024]{1,0:T(8,128)(2,1)S(1)} %pad_maximum_fusion.1), channel_id=1, source_target_pairs={{1,0},{2,1},{3,2},{4,3},{5,4},{6,5},{7,6},{8,7},{9,8},{10,9},{11,1... | collective-permute-start | bytes 393224 | tf_op jit(solution)/shard_map/ppermute | solution.py:18
  18.3 8.4 %copy-start.14 = (s32[64,16]{0,1:T(8,128)S(1)}, s32[64,16]{0,1:T(8,128)}, u32[]{:S(2)}) copy-start(s32[64,16]{0,1:T(8,128)} %param.25) | copy-start | bytes 12292
  18.3 9.6 %copy-start.16 = (s32[64,16]{0,1:T(8,128)S(1)}, s32[64,16]{0,1:T(8,128)}, u32[]{:S(2)}) copy-start(s32[64,16]{0,1:T(8,128)} %param.23) | copy-start | bytes 12292
  18.3 10.3 %copy-start.8 = (bf16[1024,512]{1,0:T(8,128)(2,1)S(1)}, bf16[1024,512]{1,0:T(8,128)(2,1)}, u32[]{:S(2)}) copy-start(bf16[1024,512]{1,0:T(8,128)(2,1)} %param.19) | copy-start | bytes 3145732
  23.3 63.9 %all-to-all-start = ((bf16[8,4,1024]{2,1,0:T(4,128)(2,1)}), bf16[8,4,1024]{2,1,0:T(4,128)(2,1)S(1)}, u32[]{:S(2)}, u32[]{:S(2)}) async-start(bf16[8,4,1024]{2,1,0:T(4,128)(2,1)} %stack.2), calls=%async_computation | async-start | bytes 131072 | tf_op jit(solution)/shard_map/all_to_all | solution.py:146
  29.2 3.6 %copy-start = (bf16[1024,512]{0,1:T(8,128)(2,1)}, bf16[1024,512]{0,1:T(8,128)(2,1)S(1)}, u32[]{:S(2)}) copy-start(bf16[1024,512]{0,1:T(8,128)(2,1)S(1)} %copy.136) | copy-start | bytes 3145732
  29.4 3.4 %copy-start.7 = (bf16[3,512,512]{2,1,0:T(8,128)(2,1)S(1)}, bf16[3,512,512]{2,1,0:T(8,128)(2,1)}, u32[]{:S(2)}) copy-start(bf16[3,512,512]{2,1,0:T(8,128)(2,1)} %param.29) | copy-start | bytes 4718596
  32.8 1.3 copy-start.17
  32.8 2.0 %copy-start.21 = (bf16[2,512]{1,0:T(2,128)(2,1)S(1)}, bf16[2,512]{1,0:T(2,128)(2,1)}, u32[]{:S(2)}) copy-start(bf16[2,512]{1,0:T(2,128)(2,1)} %param.22) | copy-start | bytes 6148
  35.0 30.6 %copy-start.4 = (f32[1024,512]{0,1:S(1)}, f32[1024,512]{0,1}, u32[]{:S(2)}) copy-start(f32[1024,512]{0,1} %get-tuple-element.40) | copy-start | bytes 6291460
  65.9 5.2 %copy-start.12 = (bf16[32,512]{1,0:T(8,128)(2,1)S(1)}, bf16[32,512]{1,0:T(8,128)(2,1)}, u32[]{:S(2)}) copy-start(bf16[32,512]{1,0:T(8,128)(2,1)} %get-tuple-element.19) | copy-start | bytes 98308
  112.0 7.6 %copy-start.13 = (pred[64,16]{1,0:T(8,128)(4,1)S(1)}, pred[64,16]{1,0:T(8,128)(4,1)}, u32[]{:S(2)}) copy-start(pred[64,16]{1,0:T(8,128)(4,1)} %copy.140) | copy-start | bytes 3076
  119.7 3.5 %copy-start.20 = (f32[8]{0:T(128)S(1)}, f32[8]{0:T(128)}, u32[]{:S(2)}) copy-start(f32[8]{0:T(128)} %get-tuple-element.35) | copy-start | bytes 100
  124.7 1.7 %copy-start.1 = (bf16[1024,512]{0,1:T(8,128)(2,1)S(1)}, bf16[1024,512]{0,1:T(8,128)(2,1)}, u32[]{:S(2)}) copy-start(bf16[1024,512]{0,1:T(8,128)(2,1)} %copy-done) | copy-start | bytes 3145732
  124.7 1.7 %copy-start.11 = (bf16[1,512,512]{2,1,0:T(8,128)(2,1)S(1)}, bf16[1,512,512]{2,1,0:T(8,128)(2,1)}, u32[]{:S(2)}) copy-start(bf16[1,512,512]{2,1,0:T(8,128)(2,1)} %get-tuple-element.12) | copy-start | bytes 1572868
  126.4 1.4 copy-start.15
  127.7 2.3 %copy-start.2 = (f32[1024,512]{0,1:T(8,128)}, f32[1024,512]{0,1:T(8,128)S(1)}, u32[]{:S(2)}) copy-start(f32[1024,512]{0,1:T(8,128)S(1)} %get-tuple-element.46) | copy-start | bytes 6291460
  130.3 1.1 copy-start.18
  130.3 1.1 copy-start.23
  131.5 4.3 %copy-start.6 = (bf16[1024,8,64]{2,1,0:T(8,128)(2,1)S(1)}, bf16[1024,8,64]{2,1,0:T(8,128)(2,1)}, u32[]{:S(2)}) copy-start(bf16[1024,8,64]{2,1,0:T(8,128)(2,1)} %gather_fusion.3) | copy-start | bytes 3145732
  135.8 2.3 %copy-start.3 = (f32[1024,512]{0,1:T(8,128)S(1)}, f32[1024,512]{0,1:T(8,128)}, u32[]{:S(2)}) copy-start(f32[1024,512]{0,1:T(8,128)} %copy-done.2) | copy-start | bytes 6291460
  135.8 2.3 %copy-start.10 = (bf16[1,512,512]{2,1,0:T(8,128)(2,1)S(1)}, bf16[1,512,512]{2,1,0:T(8,128)(2,1)}, u32[]{:S(2)}) copy-start(bf16[1,512,512]{2,1,0:T(8,128)(2,1)} %get-tuple-element.13) | copy-start | bytes 1572868
  141.7 1.8 %copy-start.22 = (f32[8]{0:T(128)S(1)}, f32[8]{0:T(128)}, u32[]{:S(2)}) copy-start(f32[8]{0:T(128)} %get-tuple-element.34) | copy-start | bytes 100
  143.5 3.9 %copy-start.5 = (bf16[1024,8,64]{2,1,0:T(8,128)(2,1)S(1)}, bf16[1024,8,64]{2,1,0:T(8,128)(2,1)}, u32[]{:S(2)}) copy-start(bf16[1024,8,64]{2,1,0:T(8,128)(2,1)} %gather_fusion.5) | copy-start | bytes 3145732
  147.4 2.1 %copy-start.9 = (bf16[1,512,512]{2,1,0:T(8,128)(2,1)S(1)}, bf16[1,512,512]{2,1,0:T(8,128)(2,1)}, u32[]{:S(2)}) copy-start(bf16[1,512,512]{2,1,0:T(8,128)(2,1)} %get-tuple-element.11) | copy-start | bytes 1572868
